TPU v7x, 32 devices: a whole 2x2x4 slice. The times are simulated.
32 devices in a mesh: dp: 4 (over x, core), section: 4 (over z), expert: 2 (over y).
Axes of the slice: x: 2, y: 2, z: 4, core: 2. Of those that a mesh axis runs over, the one named last changes fastest.
Arguments:
- tokens: bfloat16 [8192, 4096], P(('dp', 'section')), may hold values from -90 to 90
- w_query: bfloat16 [4096, 2048], P(None, 'expert'), may hold values from -0.09375 to 0.09375
- w_key: bfloat16 [4096, 1024], P(None, 'expert'), may hold values from -0.09375 to 0.09375
- w_value: bfloat16 [4096, 1024], P(None, 'expert'), may hold values from -0.09375 to 0.09375
- w_out: bfloat16 [2048, 4096], P('expert'), may hold values from -0.125 to 0.125
- w_gate: bfloat16 [2, 7168, 4096], P('expert', ('dp', 'section')), may hold values from -0.09375 to 0.09375
- w_up: bfloat16 [2, 7168, 4096], P('expert', ('dp', 'section')), may hold values from -0.09375 to 0.09375
- w_down: bfloat16 [2, 7168, 4096], P('expert', ('dp', 'section')), may hold values from -0.0625 to 0.0625
- route: int32 [128, 1], P(('dp', 'section')), may hold values from 0 to 1; in each aligned block of 8 rows (0 to 7, 8 to 15, ...) at most 5 rows name the same one
- old_out: bfloat16 [128, 64, 4096], P(('dp', 'section'), 'expert'), may hold values from -6 to 6
- cotangent: bfloat16 [8192, 4096], P(('dp', 'section')), may hold values from -6 to 6
Outputs:
- joined: bfloat16 [128, 64, 4096], P(('dp', 'section'), 'expert')
- divergence: float32 [128, 64], P(('dp', 'section'), 'expert')
- grad_out_t: float32 [4096, 2048], P(('dp', 'section'), 'expert')
Inputs may be any that keep to these rules, and one draw needn't show every extreme that they name: `route`: blocks routed to experts 1 and above go to new experts. Among the 8 blocks of one replica no expert is named more than 5 times, and some replica names one expert exactly 5 times in every draw.
All inputs are finite; a program needn't handle non-finite values.
Results may differ from a plain program's by a relative error of at most 0.025.
Values may be sent and summed in bfloat16 or wider, within the bound.
A program may use at most 192 MiB of HBM per device.

v0:
```python
import functools
import math

import jax
import jax.numpy as jnp
from jax import lax
from jax.experimental import pallas as pl
from jax.experimental.pallas import tpu as pltpu
from jax.sharding import Mesh
from jax.sharding import PartitionSpec as P


HEAD_DIM = 128
BLOCK = 64
GROUP = ("outer", "section")


def attend_local(tokens, w_query, w_key, w_value):
    length = tokens.shape[0]
    key_heads = w_key.shape[1] // HEAD_DIM
    group = w_query.shape[1] // w_key.shape[1]
    queries = jnp.dot(tokens, w_query, preferred_element_type=jnp.float32).astype(jnp.bfloat16)
    queries = queries.reshape(length, key_heads, group, HEAD_DIM)
    keys = jnp.dot(tokens, w_key, preferred_element_type=jnp.float32).astype(jnp.bfloat16)
    keys = keys.reshape(length, key_heads, HEAD_DIM)
    values = jnp.dot(tokens, w_value, preferred_element_type=jnp.float32).astype(jnp.bfloat16)
    values = values.reshape(length, key_heads, HEAD_DIM)
    scores = jnp.einsum("qkgd,skd->kgqs", queries, keys, preferred_element_type=jnp.float32)
    scores = scores * (1.0 / math.sqrt(HEAD_DIM))
    query_pos = lax.broadcasted_iota(jnp.int32, (length, length), 0)
    key_pos = lax.broadcasted_iota(jnp.int32, (length, length), 1)
    scores = jnp.where(query_pos >= key_pos, scores, -jnp.inf)
    top = jnp.max(scores, axis=-1, keepdims=True)
    weights = jnp.exp(scores - top)
    probs = (weights / jnp.sum(weights, axis=-1, keepdims=True)).astype(jnp.bfloat16)
    mixed = jnp.einsum("kgqs,skd->qkgd", probs, values, preferred_element_type=jnp.float32)
    return mixed.astype(jnp.bfloat16).reshape(length, key_heads * group * HEAD_DIM)


def routing_table(routes, experts, capacity):
    number = routes.shape[0]
    same = routes[:, None] == routes[None, :]
    earlier = lax.broadcasted_iota(jnp.int32, (number, number), 1) < lax.broadcasted_iota(
        jnp.int32, (number, number), 0
    )
    slot = jnp.sum((same & earlier).astype(jnp.int32), axis=1)
    expert_hit = routes[None, :] == lax.broadcasted_iota(jnp.int32, (experts, number), 0)
    slot_hit = slot[None, :] == lax.broadcasted_iota(jnp.int32, (capacity, number), 0)
    return (expert_hit[:, None, :] & slot_hit[None, :, :]).astype(jnp.bfloat16)


def swap(value, axis):
    return lax.ppermute(value, axis, [(0, 1), (1, 0)])


def both(value, axis=0):
    if lax.axis_size("pair") == 1:
        return value
    return jnp.concatenate([value, swap(value, "pair")], axis=axis)


def pick(blocks, table):
    rows = jnp.einsum("cb,brd->crd", table, blocks, preferred_element_type=jnp.float32)
    return rows.astype(jnp.bfloat16)


def wo_gradient(cotangent, heads_out):
    length, width = cotangent.shape
    outer, pair = lax.axis_size("outer"), lax.axis_size("pair")
    parts = cotangent.reshape(length, outer, pair, width // (outer * pair))
    mine = lax.axis_index("pair")

    def part(number):
        return lax.dynamic_index_in_dim(parts, number, 2, keepdims=False).reshape(length, width // pair)

    left = part(mine)
    if pair == 2:
        left = jnp.concatenate([left, swap(part(1 - mine), "pair")], axis=0)
    term = lax.dot_general(
        left, both(heads_out), (((0,), (0,)), ((), ())), preferred_element_type=jnp.float32
    ).astype(jnp.bfloat16)
    return lax.psum_scatter(term, GROUP, scatter_dimension=0, tiled=True).astype(jnp.float32)


def per_device(
    tokens, w_query, w_key, w_value, w_out, w_gate, w_up, w_down, route, old_out, cotangent
):
    experts = lax.axis_size("expert")
    own = lax.axis_index("expert")
    length, width = tokens.shape
    blocks = length // BLOCK
    piece_rows = BLOCK // experts
    capacity = max(2, blocks // experts + 1)
    old_count = experts - max(1, experts // 4)
    routes = route[:, 0]
    table = routing_table(routes, experts, capacity)
    own_table = lax.dynamic_index_in_dim(table, own, 0, keepdims=False)
    token_rows = pick(tokens.reshape(blocks, BLOCK, width), own_table)

    heads_out = attend_local(tokens, w_query, w_key, w_value)
    head_blocks = heads_out.reshape(blocks, BLOCK, heads_out.shape[1])

    def project(rows):
        return jnp.dot(
            rows.reshape(-1, rows.shape[-1]), w_out, preferred_element_type=jnp.float32
        ).reshape(rows.shape[:-1] + (width,))

    if experts == 2:
        half = capacity * BLOCK // 2
        peer_table = lax.dynamic_index_in_dim(table, 1 - own, 0, keepdims=False)
        outgoing = project(pick(head_blocks, peer_table)).astype(jnp.bfloat16).reshape(-1, width)
        kept = project(pick(head_blocks, own_table)).reshape(-1, width)
        kept = kept + token_rows.reshape(-1, width).astype(jnp.float32)
        first = (kept[:half] + swap(outgoing[:half], "expert").astype(jnp.float32)).astype(jnp.bfloat16)
        second = (kept[half:] + swap(outgoing[half:], "expert").astype(jnp.float32)).astype(jnp.bfloat16)
    else:
        half = capacity * BLOCK // 2
        rows = jnp.einsum("jcb,brd->jcrd", table, head_blocks, preferred_element_type=jnp.float32)
        outgoing = project(rows.astype(jnp.bfloat16)).astype(jnp.bfloat16)
        total = lax.psum_scatter(outgoing, "expert", scatter_dimension=0, tiled=True)[0]
        total = (token_rows.astype(jnp.float32) + total.astype(jnp.float32)).astype(jnp.bfloat16)
        total = total.reshape(-1, width)
        first, second = total[:half], total[half:]

    gradient = wo_gradient(cotangent, heads_out)
    gate_rows, up_rows, down_rows = both(w_gate[0]), both(w_up[0]), both(w_down[0])
    contract = (((1,), (1,)), ((), ()))

    def expert(top, bottom):
        rows = jnp.concatenate([top, bottom], axis=0)
        gate = lax.dot_general(rows, gate_rows, contract, preferred_element_type=jnp.float32)
        lifted = lax.dot_general(rows, up_rows, contract, preferred_element_type=jnp.float32)
        active = (jax.nn.silu(gate) * lifted).astype(jnp.bfloat16)
        return jnp.dot(active, down_rows, preferred_element_type=jnp.float32)

    outer, section = lax.axis_size("outer"), lax.axis_size("section")
    ring = []
    for line in range(outer):
        places = [line * section + place for place in range(section)]
        ring += places if line % 2 == 0 else places[::-1]
    count = len(ring)
    onward = [(ring[i], ring[(i + 1) % count]) for i in range(count)]
    backward = [(target, source) for source, target in onward]
    front, back = first, second
    sums = None
    for _ in range(count - 1):
        front = lax.ppermute(front, GROUP, onward)
        back = lax.ppermute(back, GROUP, backward)
        terms = expert(front, back)
        upper, lower = terms[:half], terms[half:]
        if sums is not None:
            upper = upper + lax.ppermute(sums[0], GROUP, onward).astype(jnp.float32)
            lower = lower + lax.ppermute(sums[1], GROUP, backward).astype(jnp.float32)
        sums = (upper.astype(jnp.bfloat16), lower.astype(jnp.bfloat16))
    terms = expert(first, second)
    upper = terms[:half] + lax.ppermute(sums[0], GROUP, onward).astype(jnp.float32)
    lower = terms[half:] + lax.ppermute(sums[1], GROUP, backward).astype(jnp.float32)
    expert_sum = jnp.concatenate([upper, lower], axis=0)
    hidden = jnp.concatenate([first, second], axis=0).astype(jnp.float32)
    whole = (hidden + expert_sum.astype(jnp.bfloat16).astype(jnp.float32)).astype(jnp.bfloat16)
    whole = whole.reshape(capacity, experts, piece_rows, width)
    if experts == 2:
        mine = lax.dynamic_index_in_dim(whole, own, 1, keepdims=False)
        theirs = swap(lax.dynamic_index_in_dim(whole, 1 - own, 1, keepdims=False), "expert")
        joined = jnp.einsum("cb,crd->brd", own_table, mine, preferred_element_type=jnp.float32)
        joined = joined + jnp.einsum("cb,crd->brd", peer_table, theirs, preferred_element_type=jnp.float32)
    else:
        returned = lax.all_to_all(
            whole.transpose(1, 0, 2, 3), "expert", split_axis=0, concat_axis=0, tiled=True
        )
        joined = jnp.einsum("jcb,jcrd->brd", table, returned, preferred_element_type=jnp.float32)
    joined = joined.astype(jnp.bfloat16)
    fresh = (routes >= old_count).astype(jnp.float32)
    gap = joined.astype(jnp.float32) - old_out.astype(jnp.float32)
    divergence = 0.5 * jnp.mean(gap * gap, axis=-1) * fresh[:, None]
    return (joined, divergence, gradient)


MESH_ID = pl.DeviceIdType.MESH
NT = (((1,), (1,)), ((), ()))


def moe_kernel(
    sure, loose, half,
    parcel_ref, kept_ref, early_ref, gate_ref, up_ref, down_ref, term_ref, flag_ref,
    out_ref, grad_ref, far_ref, slot_ref,
    near_w, rows, sums, stage, stage_rest, part, far_act, act, gate_tile, up_tile, grad_in, term_in, grad_out, total_grad,
    kept_in, flags,
    row_send, row_recv, sum_send, sum_recv, grad_send, grad_recv, rest_send, rest_recv,
    pair_send, pair_recv, far_send, far_recv, fwd_send, fwd_recv, got_send, got_recv, flag_send, flag_recv,
    local_sem, free_sem,
):
    outer, section = lax.axis_size("outer"), lax.axis_size("section")
    count = outer * section
    x, z = lax.axis_index("outer"), lax.axis_index("section")
    spot = x * (count - 1) + z * (1 - 2 * x)

    def at(place):
        line = place // section
        within = place % section
        return {"outer": line, "section": within * (1 - 2 * line) + (section - 1) * line}

    onward, backward = at((spot + 1) % count), at((spot + count - 1) % count)
    partner = {"pair": 1 - lax.axis_index("pair")}
    peer = {"expert": 1 - lax.axis_index("expert")}
    ways = (onward, backward)
    total_rows, width = rows.shape[1:]
    side = total_rows // 2
    block = part.shape[1]
    layers = side // block
    wide = width // 2
    rest = side - sure
    tile = half
    tiles = near_w.shape[1] * near_w.shape[2] // tile
    per = near_w.shape[2] // tile
    chunk = 512
    weights = (gate_ref, up_ref, down_ref)

    barrier = pltpu.get_barrier_semaphore()
    for target in (onward, backward, partner, peer):
        pl.semaphore_signal(barrier, inc=1, device_id=target, device_id_type=MESH_ID)
    pl.semaphore_wait(barrier, 4)

    def remote(source, target, send, recv, device):
        return pltpu.make_async_remote_copy(
            src_ref=source, dst_ref=target, send_sem=send, recv_sem=recv, device_id=device, device_id_type=MESH_ID
        )

    def span(way):
        return pl.ds(way * side, side)

    def row_copy(way, piece, step):
        columns = pl.ds(piece * wide, wide)
        return remote(
            rows.at[step - 1, span(way), columns],
            rows.at[step, span(way), columns],
            row_send.at[way, piece, step],
            row_recv.at[way, piece, step],
            ways[way],
        )

    def flag_copy(way, step):
        return remote(
            flags.at[way, step - 1], flags.at[way, step], flag_send.at[way, step], flag_recv.at[way, step], ways[way]
        )

    def got_copy(way, piece):
        here = (pl.ds(way * layers, layers), slice(None), pl.ds(piece * wide, wide))
        return remote(parcel_ref.at[here], part.at[here], got_send.at[way, piece], got_recv.at[way, piece], peer)

    high, deep = grad_in.shape[1], grad_in.shape[2]

    def term_at(way, index):
        place = (spot + index) % count
        line = place // section
        within = place % section
        block = line * section + within * (1 - 2 * line) + (section - 1) * line
        return term_ref.at[pl.ds(pl.multiple_of(block * high, high), high), pl.ds(way * deep, deep)]

    def grad_copy(way, step, source):
        return remote(source, slot_ref.at[way, step], grad_send.at[way, step], grad_recv.at[way, step], ways[way])

    def sum_copy(way, step):
        here = pl.ds(way * sure, sure)
        return remote(stage.at[step % 2, here], sums.at[step, here], sum_send.at[way, step], sum_recv.at[way, step], ways[way])

    def rest_copy(way, half_index, step):
        here = pl.ds(way * rest, rest)
        there = pl.ds(sure + way * rest, rest)
        columns = pl.ds(half_index * (width // 2), width // 2)
        return remote(
            stage_rest.at[step % 2, here, columns],
            rows.at[step, there, columns],
            rest_send.at[way, half_index, step],
            rest_recv.at[way, half_index, step],
            ways[way],
        )

    late = pl.ds(tile, near_w.shape[2] - tile)
    head = pl.ds(0, tile)

    def far_copy(which):
        source, target = weights[which], far_ref.at[which, 0]
        if which == 0:
            source, target = source.at[late], target.at[late]
        return remote(source, target, far_send.at[which], far_recv.at[which], peer)

    def forward_copy(which):
        source, target = far_ref.at[which, 0], far_ref.at[which, 1]
        if which == 0:
            source, target = source.at[late], target.at[late]
        return remote(source, target, fwd_send.at[which], fwd_recv.at[which], partner)

    def early_copy():
        return remote(early_ref, far_ref.at[0, 1, head], fwd_send.at[3], fwd_recv.at[3], partner)

    def pair_copy(which):
        return remote(weights[which], near_w.at[which, 1], pair_send.at[which], pair_recv.at[which], partner)

    def local(source, target, place):
        return pltpu.make_async_copy(source, target, local_sem.at[place])

    def gradient_step(step):
        pulls = []
        for way in range(2):
            grad_copy(way, step, slot_ref.at[way, step]).wait_recv()
            pulls.append(local(slot_ref.at[way, step], grad_in.at[way], way))
            index = (2 * count - 1 - step) % count if way == 0 else (1 + step) % count
            pulls.append(local(term_at(way, index), term_in.at[way], 2 + way))
        for pull in pulls:
            pull.start()
        for pull in pulls:
            pull.wait()
        for way in range(2):
            value = grad_in[way].astype(jnp.float32) + term_in[way].astype(jnp.float32)

            step = jnp.asarray(step, jnp.int32)

            @pl.when(step < count - 1)
            def _():
                @pl.when(step >= 3)
                def _():
                    grad_copy(way, step - 1, grad_out.at[way, step % 2]).wait_send()

                grad_out[way, step % 2] = value.astype(jnp.bfloat16)
                grad_copy(way, step + 1, grad_out.at[way, step % 2]).start()

            @pl.when(step == count - 1)
            def _():
                total_grad[:, pl.ds(way * value.shape[1], value.shape[1])] = value

    for piece in range(2):
        for way in range(2):
            got_copy(way, piece).start()
    for which in range(3):
        far_copy(which).start()
    grad_copy(0, 1, term_at(0, count - 1)).start()
    grad_copy(1, 1, term_at(1, 1)).start()
    marks = [local(flag_ref, flags.at[way, 0], way) for way in range(2)]
    for mark in marks:
        mark.start()
    for mark in marks:
        mark.wait()
    for way in range(2):
        flag_copy(way, 1).start()
    loads = [local(weights[which], near_w.at[which, 0], 1 + which) for which in range(3)]
    for load in loads:
        load.start()
    for which in range(3):
        pair_copy(which).start()
    early_copy().start()
    for load in loads:
        load.wait()
    for number in range(4):
        piece, way = number // 2, number % 2
        columns = pl.ds(piece * wide, wide)
        pull = local(kept_ref.at[pl.ds(way * layers, layers), :, columns], kept_in, 0)
        pull.start()
        pull.wait()
        got_copy(way, piece).wait_recv()

        def join(index, _):
            place = pl.ds(pl.multiple_of(way * side + index * block, block), block)
            value = kept_in[index] + part[way * layers + index, :, columns].astype(jnp.float32)
            rows[0, place, columns] = value.astype(jnp.bfloat16)
            return 0

        lax.fori_loop(0, layers, join, 0)
        row_copy(way, piece, 1).start()
        if number < 3:
            gradient_step(number + 1)
    for which in range(3):
        pair_copy(which).wait_recv()

    def gated(value, gate, up):
        pre = lax.dot_general(value, gate, NT, preferred_element_type=jnp.float32)
        lifted = lax.dot_general(value, up, NT, preferred_element_type=jnp.float32)
        return pre * (1.0 / (1.0 + jnp.exp(-pre))) * lifted

    def near_step(step):
        slot = step

        def one(index, _):
            place = pl.ds(pl.multiple_of((index % per) * tile, tile), tile)
            value = gated(rows[slot], near_w[0, index // per, place], near_w[1, index // per, place])
            act[index] = value.astype(jnp.bfloat16)
            return 0

        lax.fori_loop(0, tiles, one, 0)

        @pl.when(step >= 2)
        def _():
            for way in range(2):
                sum_copy(way, step - 1).wait_recv()

        @pl.when(step >= 3)
        def _():
            for way in range(2):
                sum_copy(way, step - 2).wait_send()

        def two(index, _):
            columns = pl.ds(pl.multiple_of(index * chunk, chunk), chunk)
            total = None
            for number in range(tiles):
                place = pl.ds((number % per) * tile, tile)
                term = jnp.dot(
                    act[number], near_w[2, number // per, place, columns], preferred_element_type=jnp.float32
                )
                total = term if total is None else total + term
            before = sums[jnp.maximum(step - 1, 0), :, columns].astype(jnp.float32)
            before = jnp.where(step >= 2, before, 0.0)
            stage[step % 2, 0:sure, columns] = (total[0:sure] + before[0:sure]).astype(jnp.bfloat16)
            stage[step % 2, sure : 2 * sure, columns] = (total[total_rows - sure :] + before[sure:]).astype(jnp.bfloat16)
            part[slot, 0:loose, columns] = jnp.where(
                flags[0, slot][:, 0:1] > 0, total[sure : sure + loose], 0.0
            ).astype(jnp.bfloat16)
            part[slot, loose : 2 * loose, columns] = jnp.where(
                flags[1, slot][:, 0:1] > 0, total[side : side + loose], 0.0
            ).astype(jnp.bfloat16)
            return 0

        lax.fori_loop(0, width // chunk, two, 0)

    def far_step(low, high):
        def one(index, _):
            place = pl.ds(pl.multiple_of((index % per) * tile, tile), tile)
            gate_fetch = local(far_ref.at[0, index // per, place], gate_tile, 0)
            up_fetch = local(far_ref.at[1, index // per, place], up_tile, 1)

            @pl.when(index == 0)
            def _():
                fetch = local(early_ref, gate_tile, 0)
                fetch.start()
                fetch.wait()

            up_fetch.start()

            @pl.when(index > 0)
            def _():
                gate_fetch.start()
                gate_fetch.wait()

            up_fetch.wait()

            def two(step, _):
                slot = step % count
                value = gated(rows[slot, sure : sure + 2 * rest], gate_tile[...], up_tile[...])
                for way in range(2):
                    base = way * rest
                    far_act[slot, index, base : base + loose] = jnp.where(
                        flags[way, slot][:, 0:1] > 0, 0.0, value[base : base + loose]
                    ).astype(jnp.bfloat16)
                    far_act[slot, index, base + loose : base + rest] = value[base + loose : base + rest].astype(
                        jnp.bfloat16
                    )
                return 0

            lax.fori_loop(low, high, two, 0)
            return 0

        lax.fori_loop(0, tiles, one, 0)

    def ring_step(step, _):
        @pl.when(step >= 1)
        def _():
            for piece in range(2):
                for way in range(2):
                    row_copy(way, piece, step).wait_recv()

                    @pl.when(step < count - 1)
                    def _():
                        row_copy(way, piece, step + 1).start()

            for way in range(2):
                flag_copy(way, step).wait_recv()

                @pl.when(step < count - 1)
                def _():
                    flag_copy(way, step + 1).start()

        @pl.when((step >= 1) & (step < count - 3))
        def _():
            gradient_step(step + 3)

        near_step(step)

        @pl.when(step >= 1)
        def _():
            for way in range(2):
                sum_copy(way, step).start()

        @pl.when(step == 0)
        def _():
            sums[0] = stage[0]

        for which, when in ((0, count // 2 - 1), (1, count - 3), (2, count - 1)):
            @pl.when(step == when)
            def _():
                far_copy(which).wait_recv()
                forward_copy(which).start()

        @pl.when(step == count - 3)
        def _():
            early_copy().wait_recv()
            for which in range(2):
                forward_copy(which).wait_recv()

        @pl.when((step >= count - 3) & (step < count - 1))
        def _():
            low = 3 * (step - (count - 3))
            far_step(low, low + 3)

        return 0

    lax.fori_loop(0, count, ring_step, 0)

    for way in range(2):
        for step in range(1, count):
            flag_copy(way, step).wait_send()
            for piece in range(2):
                row_copy(way, piece, step).wait_send()

    def grant(turn):
        pl.semaphore_signal(free_sem.at[0, turn], inc=1, device_id=backward, device_id_type=MESH_ID)
        pl.semaphore_signal(free_sem.at[1, turn], inc=1, device_id=onward, device_id_type=MESH_ID)

    grant(0)
    pulls = [local(far_ref.at[2, 0], near_w.at[0, 0], 0), local(far_ref.at[2, 1], near_w.at[0, 1], 1)]
    pulls[0].start()
    forward_copy(2).wait_recv()
    pulls[1].start()
    for pull in pulls:
        pull.wait()

    def rest_step(step, _):
        slot = step % count

        def two(index, _):
            columns = pl.ds(pl.multiple_of(index * chunk, chunk), chunk)
            total = None
            for number in range(tiles):
                place = pl.ds((number % per) * tile, tile)
                term = jnp.dot(
                    far_act[slot, number], near_w[0, number // per, place, columns], preferred_element_type=jnp.float32
                )
                total = term if total is None else total + term
            piece = part[slot, :, columns].astype(jnp.float32)
            for way in range(2):
                base = way * rest
                near_w[1, 0, base : base + loose, columns] = (
                    total[base : base + loose] + piece[way * loose : (way + 1) * loose]
                ).astype(jnp.bfloat16)
                near_w[1, 0, base + loose : base + rest, columns] = total[base + loose : base + rest].astype(jnp.bfloat16)
            return 0

        lax.fori_loop(0, width // chunk, two, 0)

        for turn, when in ((0, 1), (1, count - 2)):
            @pl.when(step == when)
            def _():
                for way in range(2):
                    pl.semaphore_wait(free_sem.at[way, turn], 1)

        for half_index in range(2):
            for way in range(2):
                here = slice(way * rest, (way + 1) * rest)
                there = slice(sure + way * rest, sure + (way + 1) * rest)
                columns = slice(half_index * (width // 2), (half_index + 1) * (width // 2))

                @pl.when(step >= 3)
                def _():
                    rest_copy(way, half_index, step - 2).wait_send()

                @pl.when(step >= 2)
                def _():
                    rest_copy(way, half_index, step - 1).wait_recv()
                    stage_rest[step % 2, here, columns] = (
                        near_w[1, 0, here, columns].astype(jnp.float32) + rows[step - 1, there, columns].astype(jnp.float32)
                    ).astype(jnp.bfloat16)

                @pl.when(step < 2)
                def _():
                    stage_rest[step % 2, here, columns] = near_w[1, 0, here, columns]

                @pl.when(step < count)
                def _():
                    rest_copy(way, half_index, step).start()

        @pl.when(step == 1)
        def _():
            far_step(count - 2, count)
            grant(1)

        return 0

    lax.fori_loop(1, count + 1, rest_step, 0)
    for way in range(2):
        sum_copy(way, count - 1).wait_recv()

    def last(index, _):
        columns = pl.ds(pl.multiple_of(index * chunk, chunk), chunk)
        base = rows[0, :, columns].astype(jnp.float32)
        certain = sums[0, :, columns].astype(jnp.float32) + sums[count - 1, :, columns].astype(jnp.float32)
        certain = certain.astype(jnp.bfloat16).astype(jnp.float32)
        others = stage_rest[count % 2, :, columns].astype(jnp.float32)
        rows[0, 0:sure, columns] = (base[0:sure] + certain[0:sure]).astype(jnp.bfloat16)
        rows[0, sure : sure + 2 * rest, columns] = (base[sure : sure + 2 * rest] + others).astype(jnp.bfloat16)
        rows[0, total_rows - sure :, columns] = (base[total_rows - sure :] + certain[sure:]).astype(jnp.bfloat16)
        return 0

    lax.fori_loop(0, width // chunk, last, 0)
    pushes = [local(rows.at[0], out_ref, 0), local(total_grad, grad_ref, 1)]
    for push in pushes:
        push.start()
    for push in pushes:
        push.wait()
    for way in range(2):
        sum_copy(way, count - 2).wait_send()
        sum_copy(way, count - 1).wait_send()
        for half_index in range(2):
            rest_copy(way, half_index, count - 1).wait_send()
        grad_copy(way, 1, term_at(way, 0)).wait_send()
        for step in range(max(2, count - 2), count):
            grad_copy(way, step, grad_out.at[way, step % 2]).wait_send()
        for piece in range(2):
            got_copy(way, piece).wait_send()
    early_copy().wait_send()
    for which in range(3):
        pair_copy(which).wait_send()
        far_copy(which).wait_send()
        forward_copy(which).wait_send()


def attend_kernel(tokens_ref, query_ref, key_ref, value_ref, out_ref):
    tokens = tokens_ref[...]
    length = tokens.shape[0]
    low = jnp.bfloat16
    queries = jnp.dot(tokens, query_ref[...], preferred_element_type=jnp.float32).astype(low)
    keys = jnp.dot(tokens, key_ref[...], preferred_element_type=jnp.float32).astype(low)
    values = jnp.dot(tokens, value_ref[...], preferred_element_type=jnp.float32).astype(low)
    group = queries.shape[1] // keys.shape[1]
    step = 128 if length % 128 == 0 else length
    for head in range(queries.shape[1] // HEAD_DIM):
        across = slice(head * HEAD_DIM, (head + 1) * HEAD_DIM)
        shared = slice(head // group * HEAD_DIM, (head // group + 1) * HEAD_DIM)
        for start in range(0, length, step):
            end = start + step
            scores = lax.dot_general(
                queries[start:end, across], keys[:end, shared], NT, preferred_element_type=jnp.float32
            )
            scores = scores * (1.0 / math.sqrt(HEAD_DIM))
            query_pos = lax.broadcasted_iota(jnp.int32, scores.shape, 0) + start
            key_pos = lax.broadcasted_iota(jnp.int32, scores.shape, 1)
            scores = jnp.where(query_pos >= key_pos, scores, -jnp.inf)
            top = jnp.max(scores, axis=-1, keepdims=True)
            parts = jnp.exp(scores - top)
            probs = (parts / jnp.sum(parts, axis=-1, keepdims=True)).astype(low)
            mixed = jnp.dot(probs, values[:end, shared], preferred_element_type=jnp.float32)
            out_ref[start:end, across] = mixed.astype(low)


def attended(tokens, w_query, w_key, w_value):
    length, width = tokens.shape
    heads, keys = w_query.shape[1], w_key.shape[1]
    steps = 2 if keys // HEAD_DIM % 2 == 0 else 1
    wide, narrow = heads // steps, keys // steps
    return pl.pallas_call(
        attend_kernel,
        grid=(steps,),
        in_specs=[
            pl.BlockSpec((length, width), lambda i: (0, 0)),
            pl.BlockSpec((width, wide), lambda i: (0, i)),
            pl.BlockSpec((width, narrow), lambda i: (0, i)),
            pl.BlockSpec((width, narrow), lambda i: (0, i)),
        ],
        out_specs=pl.BlockSpec((length, wide), lambda i: (0, i)),
        out_shape=jax.ShapeDtypeStruct((length, heads), jnp.bfloat16),
        cost_estimate=pl.CostEstimate(
            flops=2 * length * width * (heads + 2 * keys), bytes_accessed=2 * width * (length + heads + 2 * keys), transcendentals=0
        ),
    )(tokens, w_query, w_key, w_value)


def project_kernel(
    capacity, route_ref, own_ref, heads_ref, weight_ref, tokens_ref, parcel_ref, kept_ref, place_ref, flag_ref, order_ref, picked
):
    strips, strip = order_ref.shape[1], heads_ref.shape[1]
    half = strips * strip
    blocks = strips // 2
    certain = blocks - capacity
    own = own_ref[0]

    @pl.when(pl.program_id(0) == 0)
    def _():
        routes = [route_ref[index] for index in range(blocks)]
        loose_before = jnp.int32(0)
        marks = [jnp.int32(0) for _ in range(blocks - 2 * certain)]
        for index in range(blocks):
            slot = jnp.int32(0)
            for other in range(index):
                slot = slot + jnp.where(routes[other] == routes[index], 1, 0)
            for which, first in ((0, 1 - own), (1, own)):
                fixed = jnp.where(routes[index] == first, slot, capacity + slot)
                place = jnp.where(slot >= certain, certain + loose_before, fixed)
                behind = blocks + (place + blocks - certain) % blocks
                strip_at = index * 4 + first * 2
                order_ref[which, place] = strip_at
                order_ref[which, behind] = strip_at + 1
                if which == 1:
                    place_ref[0, index] = place
                    place_ref[1, index] = behind
            for mark in range(len(marks)):
                mine = (slot >= certain) & (loose_before == mark) & (routes[index] == own)
                marks[mark] = marks[mark] + jnp.where(mine, 1, 0)
            loose_before = loose_before + jnp.where(slot >= certain, 1, 0)
        for mark, found in enumerate(marks):
            flag_ref[mark * strip : (mark + 1) * strip] = jnp.full((strip, 128), found.astype(jnp.float32))
        for which in range(2):
            for index in range(strips):
                start = which * half + index * strip
                picked[start : start + strip] = heads_ref[order_ref[which, index]]

    value = jnp.dot(picked[...], weight_ref[...], preferred_element_type=jnp.float32)
    parcel_ref[...] = value[:half].astype(jnp.bfloat16)
    for index in range(strips):
        here = slice(index * strip, (index + 1) * strip)
        kept_ref[here] = value[half + index * strip : half + (index + 1) * strip] + tokens_ref[
            order_ref[1, index]
        ].astype(jnp.float32)


def projected(routes, own, heads_out, weight, tokens, strip, capacity):
    depth, width = weight.shape
    blocks = routes.shape[0]
    count = 2 * blocks * strip
    strips = heads_out.shape[0] // strip
    free = blocks - 2 * (blocks - capacity)
    tile = 1024
    piece = pl.BlockSpec((count, tile), lambda i, route, own: (0, i))
    return pl.pallas_call(
        functools.partial(project_kernel, capacity),
        grid_spec=pltpu.PrefetchScalarGridSpec(
            num_scalar_prefetch=2,
            grid=(width // tile,),
            in_specs=[
                pl.BlockSpec((strips, strip, depth), lambda i, route, own: (0, 0, 0)),
                pl.BlockSpec((depth, tile), lambda i, route, own: (0, i)),
                pl.BlockSpec((strips, strip, tile), lambda i, route, own: (0, 0, i)),
            ],
            out_specs=[
                piece,
                piece,
                pl.BlockSpec((2, blocks), lambda i, route, own: (0, 0), memory_space=pltpu.SMEM),
                pl.BlockSpec((free * strip, 128), lambda i, route, own: (0, 0)),
            ],
            scratch_shapes=[pltpu.SMEM((2, 2 * blocks), jnp.int32), pltpu.VMEM((2 * count, depth), jnp.bfloat16)],
        ),
        out_shape=(
            jax.ShapeDtypeStruct((count, width), jnp.bfloat16),
            jax.ShapeDtypeStruct((count, width), jnp.float32),
            jax.ShapeDtypeStruct((2, blocks), jnp.int32),
            jax.ShapeDtypeStruct((free * strip, 128), jnp.float32),
        ),
        cost_estimate=pl.CostEstimate(flops=4 * count * depth * width, bytes_accessed=2 * 10**7, transcendentals=0),
    )(routes, own.reshape(1), heads_out.reshape(strips, strip, depth), weight, tokens.reshape(strips, strip, width))


def finish_kernel(place_ref, route_ref, front_ref, back_ref, old_ref, joined_ref, divergence_ref):
    strip = front_ref.shape[1]
    fresh = jnp.where(route_ref[pl.program_id(0)] >= 1, 1.0, 0.0)
    for index, source in enumerate((front_ref, back_ref)):
        here = slice(index * strip, (index + 1) * strip)
        value = source[0]
        joined_ref[0, here] = value
        gap = value.astype(jnp.float32) - old_ref[0, here].astype(jnp.float32)
        divergence_ref[0, here] = 0.5 * jnp.mean(gap * gap, axis=-1, keepdims=True) * fresh


def finished(place, fresh, out, old_out, strip):
    blocks, piece, width = old_out.shape
    whole = pl.BlockSpec((1, piece, width), lambda i, place, fresh: (i, 0, 0))
    return pl.pallas_call(
        finish_kernel,
        grid_spec=pltpu.PrefetchScalarGridSpec(
            num_scalar_prefetch=2,
            grid=(blocks,),
            in_specs=[
                pl.BlockSpec((1, strip, width), lambda i, place, fresh: (place[0, i], 0, 0)),
                pl.BlockSpec((1, strip, width), lambda i, place, fresh: (place[1, i], 0, 0)),
                whole,
            ],
            out_specs=[whole, pl.BlockSpec((1, piece, 1), lambda i, place, fresh: (i, 0, 0))],
        ),
        out_shape=(
            jax.ShapeDtypeStruct((blocks, piece, width), jnp.bfloat16),
            jax.ShapeDtypeStruct((blocks, piece, 1), jnp.float32),
        ),
    )(place, fresh, out.reshape(-1, strip, width), out.reshape(-1, strip, width), old_out)


def two_experts(
    tokens, w_query, w_key, w_value, w_out, w_gate, w_up, w_down, route, old_out, cotangent
):
    own = lax.axis_index("expert")
    length, width = tokens.shape
    blocks = length // BLOCK
    piece = BLOCK // 2
    strip = piece // 2
    capacity = max(2, blocks // 2 + 1)
    certain = blocks - capacity
    free = blocks - 2 * certain
    sure, loose, rest = certain * strip, free * strip, capacity * strip
    side = blocks * strip
    routes = route[:, 0]
    outer, section = lax.axis_size("outer"), lax.axis_size("section")
    ring = []
    for line in range(outer):
        places = [line * section + place for place in range(section)]
        ring += places if line % 2 == 0 else places[::-1]
    count = len(ring)

    early = swap(w_gate[0][: w_gate.shape[1] // 2], "expert")
    heads_out = attended(tokens, w_query, w_key, w_value)
    parcel, kept, place, flag_rows = projected(routes, own, heads_out, w_out, tokens, strip, capacity)

    core = lax.axis_index("pair")
    span = width // (outer * 2)

    def part(number):
        pieces = [
            lax.dynamic_slice_in_dim(cotangent, (line * 2 + number) * span, span, axis=1) for line in range(outer)
        ]
        return jnp.concatenate(pieces, axis=1)

    left = jnp.concatenate([part(core), swap(part(1 - core), "pair")], axis=0)
    term = lax.dot_general(
        left, both(heads_out), (((0,), (0,)), ((), ())), preferred_element_type=jnp.float32
    ).astype(jnp.bfloat16)
    high, deep = width // (2 * count), term.shape[1]

    hidden_units = w_gate.shape[1]
    half = hidden_units // 2
    tiles = 4
    any_space = pl.BlockSpec(memory_space=pl.ANY)
    low = jnp.bfloat16
    dma = pltpu.SemaphoreType.DMA
    out, gradient, _, _ = pl.pallas_call(
        functools.partial(moe_kernel, sure, loose, half),
        out_shape=(
            jax.ShapeDtypeStruct((2 * side, width), low),
            jax.ShapeDtypeStruct((high, deep), jnp.float32),
            jax.ShapeDtypeStruct((3, 2, hidden_units, width), low),
            jax.ShapeDtypeStruct((2, count, high, deep // 2), low),
        ),
        in_specs=[any_space] * 8,
        out_specs=[any_space] * 4,
        scratch_shapes=[
            pltpu.VMEM((3, 2, hidden_units, width), low),
            pltpu.VMEM((count, 2 * side, width), low),
            pltpu.VMEM((count, 2 * sure, width), low),
            pltpu.VMEM((2, 2 * sure, width), low),
            pltpu.VMEM((2, 2 * rest, width), low),
            pltpu.VMEM((count, 2 * loose, width), low),
            pltpu.VMEM((count, tiles, 2 * rest, half), low),
            pltpu.VMEM((tiles, 2 * side, half), low),
            pltpu.VMEM((half, width), low),
            pltpu.VMEM((half, width), low),
            pltpu.VMEM((2, high, deep // 2), low),
            pltpu.VMEM((2, high, deep // 2), low),
            pltpu.VMEM((2, 2, high, deep // 2), low),
            pltpu.VMEM((high, deep), jnp.float32),
            pltpu.VMEM((side // (2 * loose), 2 * loose, width // 2), jnp.float32),
            pltpu.VMEM((2, count, loose, 128), jnp.float32),
            dma((2, 2, count)), dma((2, 2, count)), dma((2, count)), dma((2, count)),
            dma((2, count)), dma((2, count)), dma((2, 2, count)), dma((2, 2, count)),
            dma((3,)), dma((3,)), dma((3,)), dma((3,)), dma((4,)), dma((4,)),
            dma((2, 2)), dma((2, 2)), dma((2, count)), dma((2, count)),
            dma((4,)), pltpu.SemaphoreType.REGULAR((2, 2)),
        ],
        compiler_params=pltpu.CompilerParams(
            collective_id=0, has_side_effects=True, vmem_limit_bytes=67043328
        ),
        cost_estimate=pl.CostEstimate(flops=10**11, bytes_accessed=10**8, transcendentals=0),
    )(
        parcel.reshape(-1, 2 * loose, width),
        kept.reshape(-1, 2 * loose, width),
        early,
        w_gate[0],
        w_up[0],
        w_down[0],
        term,
        flag_rows,
    )

    joined, divergence = finished(place, routes, out, old_out, strip)
    divergence = divergence.reshape(blocks, piece)
    return (joined, divergence, gradient)


def solution(mesh):
    sizes = mesh.shape
    pair = 2 if sizes["dp"] % 2 == 0 else 1
    replicas_in_ring = sizes["dp"] // pair * sizes["section"]
    body = two_experts if sizes["expert"] == 2 and pair == 2 and replicas_in_ring == 8 else per_device
    split = Mesh(
        mesh.devices.reshape(sizes["dp"] // pair, pair, sizes["section"], sizes["expert"]),
        ("outer", "pair", "section", "expert"),
    )
    replicas = ("outer", "pair", "section")
    return jax.shard_map(
        body,
        mesh=split,
        in_specs=(
            P(replicas, None),
            P(None, "expert"),
            P(None, "expert"),
            P(None, "expert"),
            P("expert", None),
            P("expert", replicas, None),
            P("expert", replicas, None),
            P("expert", replicas, None),
            P(replicas, None),
            P(replicas, "expert", None),
            P(replicas, None),
        ),
        out_specs=(
            P(replicas, "expert", None),
            P(replicas, "expert"),
            P(replicas, "expert"),
        ),
        check_vma=False,
    )
```

profile of v0, /device:TPU:0, one launch (start us, length us, event | category | flops | bytes accessed | tf_op | source)
XLA Modules:
  0.0 473.8 jit_solution(1728802217124220446)
XLA Ops:
  0.6 3.7 constant_dynamic-slice_fusion.3
  4.3 0.0 copy-start.1
  4.3 0.2 pad_maximum_fusion
  4.5 0.6 collective-permute-start.1
  5.0 1.3 copy-done.1
  6.3 1.4 slice_bitcast_fusion
  7.7 3.0 collective-permute-start
  10.7 23.7 %shard_map.130 = bf16[512,1024]{1,0:T(8,128)(2,1)} custom-call(bf16[512,4096]{1,0:T(8,128)(2,1)} %tokens_ref.1, bf16[4096,1024]{1,0:T(8,128)(2,1)} %query_ref.1, bf16[4096,512]{1,0:T(8,128)(2,1)} %key_ref.1, bf16[4096,512]{1,0:T(8,128)(2,1)} %value_ref.1), custom_call_target="tpu_custom_call" | custom-call | flops 8589934592 | bytes 20971520 | tf_op jit(solution)/shard_map/pallas_call | solution.py:667
  34.5 0.0 collective-permute-start.2
  34.5 10.9 %shard_map.131 = (bf16[256,4096]{1,0:T(8,128)(2,1)}, f32[256,4096]{1,0:T(8,128)}, s32[2,8]{1,0:T(2,128)}, f32[32,128]{1,0:T(8,128)}) custom-call(s32[8]{0:T(128)} %bitcast.15, s32[1]{0:T(128)} %bitcast.1.own_ref, bf16[32,16,1024]{2,1,0:T(8,128)(2,1)} %bitcast.20, bf16[1024,4096]{1,0:T(8,128)(2,1)} %weight_ref.1, bf16[32,16,4096]{2,1,0:T(8,128)(2,1)} %bitcast.17), custom_call_target="tpu_custom_call" | custom-call | flops 4294967296 | bytes 20000000 | tf_op jit(solution)/shard_map/pallas_call | solution.py:740
  45.3 0.0 collective-permute-done.2
  45.3 0.0 collective-permute-done.1
  45.3 9.1 %fusion.6.term_ref = bf16[2048,1024]{1,0:T(8,128)(2,1)} fusion(bf16[512,2048]{1,0:T(8,128)(2,1)} %collective-permute-done.1, bf16[512,1024]{1,0:T(8,128)(2,1)} %get-tuple-element.20, bf16[512,1024]{1,0:T(8,128)(2,1)S(1)} %get-tuple-element.19, bf16[512,1024]{1,0:T(8,128)(2,1)} %collective-permute-done.2, bf16[512,1024]{1,0:T(8,128)(2,1)} %shard_map.130), kind=kOutput, calls=%fused_computation.6 | convolution fusion | flops 4313841664 | bytes 10485760 | tf_op jit(solution)/shard_map/dot_general | solution.py:836
  54.5 0.0 collective-permute-done.early_ref
  54.5 409.5 %shard_map.132 = (bf16[256,4096]{1,0:T(8,128)(2,1)}, f32[256,1024]{1,0:T(8,128)}, bf16[3,2,448,4096]{3,2,1,0:T(8,128)(2,1)}, bf16[2,8,256,512]{3,2,1,0:T(8,128)(2,1)}) custom-call(bf16[4,64,4096]{2,1,0:T(8,128)(2,1)} %bitcast.22, f32[4,64,4096]{2,1,0:T(8,128)} %bitcast.21, bf16[224,4096]{1,0:T(8,128)(2,1)} %collective-permute-done.early_ref, ...), custom_call_target="tpu_custom_call" | custom-call | flops 99999997952 | bytes 100000000 | tf_op jit(solution)/shard_map/pallas_call | solution.py:847
  464.0 0.0 copy-start
  464.0 7.2 %shard_map.133 = (bf16[8,32,4096]{2,1,0:T(8,128)(2,1)}, f32[8,32,1]{2,1,0:T(8,128)}) custom-call(s32[2,8]{1,0:T(2,128)} %get-tuple-element.11.place_ref, s32[8]{0:T(128)} %bitcast.16, bf16[16,16,4096]{2,1,0:T(8,128)(2,1)} %bitcast.12, bf16[16,16,4096]{2,1,0:T(8,128)(2,1)} %bitcast.13, bf16[8,32,4096]{2,1,0:T(8,128)(2,1)} %old_ref.1), custom_call_target="tpu_custom_call" | custom-call | tf_op jit(solution)/shard_map/pallas_call | solution.py:782
  471.3 1.6 reduce
  472.9 0.0 copy-done
  472.9 1.0 copy.15
Async XLA Ops:
  4.3 2.0 copy-start.1
  4.5 40.9 %collective-permute-start.1 = (bf16[512,2048]{1,0:T(8,128)(2,1)S(1)}, bf16[512,2048]{1,0:T(8,128)(2,1)}, u32[]{:S(2)}, u32[]{:S(2)}) collective-permute-start(bf16[512,2048]{1,0:T(8,128)(2,1)S(1)} %pad_maximum_fusion), channel_id=1, source_target_pairs={{0,8},{8,0},{1,9},{9,1},{2,10},{10,2},{3,11},{11,3},{4,12},{12,4},... | collective-permute-start | bytes 6291464 | tf_op jit(solution)/shard_map/ppermute | solution.py:53
  7.7 46.7 %collective-permute-start = (bf16[224,4096]{1,0:T(8,128)(2,1)}, bf16[224,4096]{1,0:T(8,128)(2,1)}, u32[]{:S(2)}, u32[]{:S(2)}) collective-permute-start(bf16[224,4096]{1,0:T(8,128)(2,1)} %slice_bitcast_fusion), channel_id=1, source_target_pairs={{0,1},{1,0},{2,3},{3,2},{4,5},{5,4},{6,7},{7,6},{8,9},{9,8},{10,11... | collective-permute-start | bytes 5505032 | tf_op jit(solution)/shard_map/ppermute | solution.py:53
  34.5 10.9 %collective-permute-start.2 = (bf16[512,1024]{1,0:T(8,128)(2,1)}, bf16[512,1024]{1,0:T(8,128)(2,1)}, u32[]{:S(2)}, u32[]{:S(2)}) collective-permute-start(bf16[512,1024]{1,0:T(8,128)(2,1)} %shard_map.130), channel_id=1, source_target_pairs={{0,8},{8,0},{1,9},{9,1},{2,10},{10,2},{3,11},{11,3},{4,12},{12,4},... | collective-permute-start | bytes 3145736 | tf_op jit(solution)/shard_map/ppermute | solution.py:53
  464.0 8.8 %copy-start = (f32[256,1024]{1,0:T(8,128)S(1)}, f32[256,1024]{1,0:T(8,128)}, u32[]{:S(2)}) copy-start(f32[256,1024]{1,0:T(8,128)} %get-tuple-element.28) | copy-start | bytes 3145732
where the time goes:
time: 475 us; the launch traced here: 474 us
  Pallas kernels  451 us (95%)
  matrix products  9.13 us (2%)
  local copies, waits for them, and re-layouts  7.33 us (2%)
    pallas_call x1, Pallas kernels, two_experts(): pl.pallas_call(functools.partial(moe_kernel, sure, loose, half), out_shap...  410 us
    pallas_call x1, Pallas kernels, attended(): pl.pallas_call(attend_kernel, grid=(steps,), in_specs=[pl.BlockSpec((leng...  23.7 us
    pallas_call x1, Pallas kernels, projected(): pl.pallas_call(functools.partial(project_kernel, capacity), grid_spec=plt...  10.9 us
  transfers between devices with their start and end apart: 3, of which 0 were waited for; matrix products, arithmetic and copies ran while one was open for 2% of the time, Pallas kernels for 7%

commit v1 on v0

--- a/solution.py
+++ b/solution.py
@@ -248,17 +248,23 @@
         here = (pl.ds(way * layers, layers), slice(None), pl.ds(piece * wide, wide))
         return remote(parcel_ref.at[here], part.at[here], got_send.at[way, piece], got_recv.at[way, piece], peer)
 
-    high, deep = grad_in.shape[1], grad_in.shape[2]
-
-    def term_at(way, index):
+    high, deep = grad_in.shape[2], grad_in.shape[3]
+
+    def term_at(way, index, part_index):
         place = (spot + index) % count
         line = place // section
         within = place % section
-        block = line * section + within * (1 - 2 * line) + (section - 1) * line
+        block = (line * section + within * (1 - 2 * line) + (section - 1) * line) * 2 + part_index
         return term_ref.at[pl.ds(pl.multiple_of(block * high, high), high), pl.ds(way * deep, deep)]
 
-    def grad_copy(way, step, source):
-        return remote(source, slot_ref.at[way, step], grad_send.at[way, step], grad_recv.at[way, step], ways[way])
+    def grad_copy(way, part_index, step, source):
+        return remote(
+            source,
+            slot_ref.at[way, part_index, step],
+            grad_send.at[way, part_index, step],
+            grad_recv.at[way, part_index, step],
+            ways[way],
+        )
 
     def sum_copy(way, step):
         here = pl.ds(way * sure, sure)
@@ -301,41 +307,36 @@
         return pltpu.make_async_copy(source, target, local_sem.at[place])
 
     def gradient_step(step):
-        pulls = []
-        for way in range(2):
-            grad_copy(way, step, slot_ref.at[way, step]).wait_recv()
-            pulls.append(local(slot_ref.at[way, step], grad_in.at[way], way))
-            index = (2 * count - 1 - step) % count if way == 0 else (1 + step) % count
-            pulls.append(local(term_at(way, index), term_in.at[way], 2 + way))
-        for pull in pulls:
-            pull.start()
-        for pull in pulls:
-            pull.wait()
-        for way in range(2):
-            value = grad_in[way].astype(jnp.float32) + term_in[way].astype(jnp.float32)
-
-            step = jnp.asarray(step, jnp.int32)
-
-            @pl.when(step < count - 1)
-            def _():
-                @pl.when(step >= 3)
-                def _():
-                    grad_copy(way, step - 1, grad_out.at[way, step % 2]).wait_send()
-
-                grad_out[way, step % 2] = value.astype(jnp.bfloat16)
-                grad_copy(way, step + 1, grad_out.at[way, step % 2]).start()
-
-            @pl.when(step == count - 1)
-            def _():
-                total_grad[:, pl.ds(way * value.shape[1], value.shape[1])] = value
+        for part_index in range(2):
+            for way in range(2):
+                index = (2 * count - 1 - step) % count if way == 0 else (1 + step) % count
+                local(term_at(way, index, part_index), term_in.at[way, part_index], 4 + 2 * way + part_index).start()
+        for part_index in range(2):
+            pulls = []
+            for way in range(2):
+                grad_copy(way, part_index, step, slot_ref.at[way, part_index, step]).wait_recv()
+                pulls.append(local(slot_ref.at[way, part_index, step], grad_in.at[way, part_index], 2 * way + part_index))
+                pulls[-1].start()
+            for way in range(2):
+                pulls[way].wait()
+                local(term_at(way, 0, part_index), term_in.at[way, part_index], 4 + 2 * way + part_index).wait()
+                value = grad_in[way, part_index].astype(jnp.float32) + term_in[way, part_index].astype(jnp.float32)
+                if step < count - 1:
+                    if step >= 3:
+                        grad_copy(way, part_index, step - 1, grad_out.at[way, part_index, step % 2]).wait_send()
+                    grad_out[way, part_index, step % 2] = value.astype(jnp.bfloat16)
+                    grad_copy(way, part_index, step + 1, grad_out.at[way, part_index, step % 2]).start()
+                else:
+                    total_grad[pl.ds(part_index * high, high), pl.ds(way * deep, deep)] = value
 
     for piece in range(2):
         for way in range(2):
             got_copy(way, piece).start()
     for which in range(3):
         far_copy(which).start()
-    grad_copy(0, 1, term_at(0, count - 1)).start()
-    grad_copy(1, 1, term_at(1, 1)).start()
+    for part_index in range(2):
+        grad_copy(0, part_index, 1, term_at(0, count - 1, part_index)).start()
+        grad_copy(1, part_index, 1, term_at(1, 1, part_index)).start()
     marks = [local(flag_ref, flags.at[way, 0], way) for way in range(2)]
     for mark in marks:
         mark.start()
@@ -367,8 +368,8 @@
 
         lax.fori_loop(0, layers, join, 0)
         row_copy(way, piece, 1).start()
-        if number < 3:
-            gradient_step(number + 1)
+        for step in range(2 * number + 1, min(2 * number + 3, count)):
+            gradient_step(step)
     for which in range(3):
         pair_copy(which).wait_recv()
 
@@ -478,10 +479,6 @@
                 def _():
                     flag_copy(way, step + 1).start()
 
-        @pl.when((step >= 1) & (step < count - 3))
-        def _():
-            gradient_step(step + 3)
-
         near_step(step)
 
         @pl.when(step >= 1)
@@ -619,9 +616,10 @@
         sum_copy(way, count - 1).wait_send()
         for half_index in range(2):
             rest_copy(way, half_index, count - 1).wait_send()
-        grad_copy(way, 1, term_at(way, 0)).wait_send()
-        for step in range(max(2, count - 2), count):
-            grad_copy(way, step, grad_out.at[way, step % 2]).wait_send()
+        for part_index in range(2):
+            grad_copy(way, part_index, 1, term_at(way, 0, part_index)).wait_send()
+            for step in range(max(2, count - 2), count):
+                grad_copy(way, part_index, step, grad_out.at[way, part_index, step % 2]).wait_send()
         for piece in range(2):
             got_copy(way, piece).wait_send()
     early_copy().wait_send()
@@ -765,37 +763,30 @@
     )(routes, own.reshape(1), heads_out.reshape(strips, strip, depth), weight, tokens.reshape(strips, strip, width))
 
 
-def finish_kernel(place_ref, route_ref, front_ref, back_ref, old_ref, joined_ref, divergence_ref):
-    strip = front_ref.shape[1]
-    fresh = jnp.where(route_ref[pl.program_id(0)] >= 1, 1.0, 0.0)
-    for index, source in enumerate((front_ref, back_ref)):
-        here = slice(index * strip, (index + 1) * strip)
-        value = source[0]
-        joined_ref[0, here] = value
-        gap = value.astype(jnp.float32) - old_ref[0, here].astype(jnp.float32)
-        divergence_ref[0, here] = 0.5 * jnp.mean(gap * gap, axis=-1, keepdims=True) * fresh
-
-
-def finished(place, fresh, out, old_out, strip):
+def finish_kernel(place_ref, route_ref, out_ref, old_ref, joined_ref, divergence_ref):
+    blocks, strip = old_ref.shape[0], out_ref.shape[1]
+    for block in range(blocks):
+        fresh = jnp.where(route_ref[block] >= 1, 1.0, 0.0)
+        for index in range(2):
+            here = slice(index * strip, (index + 1) * strip)
+            value = out_ref[place_ref[index, block]]
+            joined_ref[block, here] = value
+            gap = value.astype(jnp.float32) - old_ref[block, here].astype(jnp.float32)
+            divergence_ref[block, here] = 0.5 * jnp.mean(gap * gap, axis=-1, keepdims=True) * fresh
+
+
+def finished(place, routes, out, old_out, strip):
     blocks, piece, width = old_out.shape
-    whole = pl.BlockSpec((1, piece, width), lambda i, place, fresh: (i, 0, 0))
+    smem, vmem = pl.BlockSpec(memory_space=pltpu.SMEM), pl.BlockSpec(memory_space=pltpu.VMEM)
     return pl.pallas_call(
         finish_kernel,
-        grid_spec=pltpu.PrefetchScalarGridSpec(
-            num_scalar_prefetch=2,
-            grid=(blocks,),
-            in_specs=[
-                pl.BlockSpec((1, strip, width), lambda i, place, fresh: (place[0, i], 0, 0)),
-                pl.BlockSpec((1, strip, width), lambda i, place, fresh: (place[1, i], 0, 0)),
-                whole,
-            ],
-            out_specs=[whole, pl.BlockSpec((1, piece, 1), lambda i, place, fresh: (i, 0, 0))],
-        ),
+        in_specs=[smem, smem, vmem, vmem],
+        out_specs=[vmem, vmem],
         out_shape=(
             jax.ShapeDtypeStruct((blocks, piece, width), jnp.bfloat16),
             jax.ShapeDtypeStruct((blocks, piece, 1), jnp.float32),
         ),
-    )(place, fresh, out.reshape(-1, strip, width), out.reshape(-1, strip, width), old_out)
+    )(place, routes, out.reshape(-1, strip, width), old_out)
 
 
 def two_experts(
@@ -850,7 +841,7 @@
             jax.ShapeDtypeStruct((2 * side, width), low),
             jax.ShapeDtypeStruct((high, deep), jnp.float32),
             jax.ShapeDtypeStruct((3, 2, hidden_units, width), low),
-            jax.ShapeDtypeStruct((2, count, high, deep // 2), low),
+            jax.ShapeDtypeStruct((2, 2, count, high // 2, deep // 2), low),
         ),
         in_specs=[any_space] * 8,
         out_specs=[any_space] * 4,
@@ -865,17 +856,17 @@
             pltpu.VMEM((tiles, 2 * side, half), low),
             pltpu.VMEM((half, width), low),
             pltpu.VMEM((half, width), low),
-            pltpu.VMEM((2, high, deep // 2), low),
-            pltpu.VMEM((2, high, deep // 2), low),
-            pltpu.VMEM((2, 2, high, deep // 2), low),
+            pltpu.VMEM((2, 2, high // 2, deep // 2), low),
+            pltpu.VMEM((2, 2, high // 2, deep // 2), low),
+            pltpu.VMEM((2, 2, 2, high // 2, deep // 2), low),
             pltpu.VMEM((high, deep), jnp.float32),
             pltpu.VMEM((side // (2 * loose), 2 * loose, width // 2), jnp.float32),
             pltpu.VMEM((2, count, loose, 128), jnp.float32),
             dma((2, 2, count)), dma((2, 2, count)), dma((2, count)), dma((2, count)),
-            dma((2, count)), dma((2, count)), dma((2, 2, count)), dma((2, 2, count)),
+            dma((2, 2, count)), dma((2, 2, count)), dma((2, 2, count)), dma((2, 2, count)),
             dma((3,)), dma((3,)), dma((3,)), dma((3,)), dma((4,)), dma((4,)),
             dma((2, 2)), dma((2, 2)), dma((2, count)), dma((2, count)),
-            dma((4,)), pltpu.SemaphoreType.REGULAR((2, 2)),
+            dma((8,)), pltpu.SemaphoreType.REGULAR((2, 2)),
         ],
         compiler_params=pltpu.CompilerParams(
             collective_id=0, has_side_effects=True, vmem_limit_bytes=67043328

time: 475 us -> 487 us (1.025)
  Pallas kernels: 451 us -> 464 us
    pallas_call x1, Pallas kernels: 410 us -> 425 us  [two_experts(): pl.pallas_call(functools.partial(moe_kernel, sure, loose, half), out_shap...]
where the time goes in v1:
time: 487 us; the launch traced here: 486 us
  Pallas kernels  464 us (95%)
  matrix products  9.13 us (2%)
  local copies, waits for them, and re-layouts  7.33 us (2%)
    pallas_call x1, Pallas kernels, two_experts(): pl.pallas_call(functools.partial(moe_kernel, sure, loose, half), out_shap...  425 us
    pallas_call x1, Pallas kernels, attended(): pl.pallas_call(attend_kernel, grid=(steps,), in_specs=[pl.BlockSpec((leng...  23.6 us
    pallas_call x1, Pallas kernels, projected(): pl.pallas_call(functools.partial(project_kernel, capacity), grid_spec=plt...  10.9 us
  transfers between devices with their start and end apart: 3, of which 0 were waited for; matrix products, arithmetic and copies ran while one was open for 2% of the time, Pallas kernels for 7%

profile of v1, /device:TPU:0, one launch (start us, length us, event | category | flops | bytes accessed | tf_op | source)
XLA Modules:
  0.0 486.1 jit_solution(8432292565987277818)
XLA Ops:
  0.6 3.7 constant_dynamic-slice_fusion.3
  4.3 0.0 copy-start.1
  4.3 0.2 pad_maximum_fusion
  4.5 0.6 collective-permute-start.1
  5.0 1.3 copy-done.1
  6.3 1.4 slice_bitcast_fusion
  7.7 3.0 collective-permute-start
  10.7 23.6 %shard_map.130 = bf16[512,1024]{1,0:T(8,128)(2,1)} custom-call(bf16[512,4096]{1,0:T(8,128)(2,1)} %tokens_ref.1, bf16[4096,1024]{1,0:T(8,128)(2,1)} %query_ref.1, bf16[4096,512]{1,0:T(8,128)(2,1)} %key_ref.1, bf16[4096,512]{1,0:T(8,128)(2,1)} %value_ref.1), custom_call_target="tpu_custom_call" | custom-call | flops 8589934592 | bytes 20971520 | tf_op jit(solution)/shard_map/pallas_call | solution.py:665
  34.3 0.0 collective-permute-start.2
  34.3 10.9 %shard_map.131 = (bf16[256,4096]{1,0:T(8,128)(2,1)}, f32[256,4096]{1,0:T(8,128)}, s32[2,8]{1,0:T(2,128)}, f32[32,128]{1,0:T(8,128)}) custom-call(s32[8]{0:T(128)} %bitcast.14, s32[1]{0:T(128)} %bitcast.1.own_ref, bf16[32,16,1024]{2,1,0:T(8,128)(2,1)} %bitcast.19, bf16[1024,4096]{1,0:T(8,128)(2,1)} %weight_ref.1, bf16[32,16,4096]{2,1,0:T(8,128)(2,1)} %bitcast.16), custom_call_target="tpu_custom_call" | custom-call | flops 4294967296 | bytes 20000000 | tf_op jit(solution)/shard_map/pallas_call | solution.py:738
  45.2 0.0 collective-permute-done.2
  45.2 0.0 collective-permute-done.1
  45.2 9.1 %fusion.6.term_ref = bf16[2048,1024]{1,0:T(8,128)(2,1)} fusion(bf16[512,2048]{1,0:T(8,128)(2,1)} %collective-permute-done.1, bf16[512,1024]{1,0:T(8,128)(2,1)} %get-tuple-element.20, bf16[512,1024]{1,0:T(8,128)(2,1)S(1)} %get-tuple-element.19, bf16[512,1024]{1,0:T(8,128)(2,1)} %collective-permute-done.2, bf16[512,1024]{1,0:T(8,128)(2,1)} %shard_map.130), kind=kOutput, calls=%fused_computation.6 | convolution fusion | flops 4313841664 | bytes 10485760 | tf_op jit(solution)/shard_map/dot_general | solution.py:827
  54.3 0.0 collective-permute-done.early_ref
  54.3 424.9 %shard_map.132 = (bf16[256,4096]{1,0:T(8,128)(2,1)}, f32[256,1024]{1,0:T(8,128)}, bf16[3,2,448,4096]{3,2,1,0:T(8,128)(2,1)}, bf16[2,2,8,128,512]{4,3,2,1,0:T(8,128)(2,1)}) custom-call(bf16[4,64,4096]{2,1,0:T(8,128)(2,1)} %bitcast.21, f32[4,64,4096]{2,1,0:T(8,128)} %bitcast.20, bf16[224,4096]{1,0:T(8,128)(2,1)} %collective-permute-done.early_ref, ...), custom_call_target="tpu_custom_call" | custom-call | flops 99999997952 | bytes 100000000 | tf_op jit(solution)/shard_map/pallas_call | solution.py:838
  479.2 0.0 copy-start
  479.2 4.3 shard_map.133
  483.5 1.6 reduce
  485.1 0.0 copy-done
  485.1 1.0 copy.15
Async XLA Ops:
  4.3 2.0 copy-start.1
  4.5 40.7 %collective-permute-start.1 = (bf16[512,2048]{1,0:T(8,128)(2,1)S(1)}, bf16[512,2048]{1,0:T(8,128)(2,1)}, u32[]{:S(2)}, u32[]{:S(2)}) collective-permute-start(bf16[512,2048]{1,0:T(8,128)(2,1)S(1)} %pad_maximum_fusion), channel_id=1, source_target_pairs={{0,8},{8,0},{1,9},{9,1},{2,10},{10,2},{3,11},{11,3},{4,12},{12,4},... | collective-permute-start | bytes 6291464 | tf_op jit(solution)/shard_map/ppermute | solution.py:53
  7.7 46.6 %collective-permute-start = (bf16[224,4096]{1,0:T(8,128)(2,1)}, bf16[224,4096]{1,0:T(8,128)(2,1)}, u32[]{:S(2)}, u32[]{:S(2)}) collective-permute-start(bf16[224,4096]{1,0:T(8,128)(2,1)} %slice_bitcast_fusion), channel_id=1, source_target_pairs={{0,1},{1,0},{2,3},{3,2},{4,5},{5,4},{6,7},{7,6},{8,9},{9,8},{10,11... | collective-permute-start | bytes 5505032 | tf_op jit(solution)/shard_map/ppermute | solution.py:53
  34.3 10.9 %collective-permute-start.2 = (bf16[512,1024]{1,0:T(8,128)(2,1)}, bf16[512,1024]{1,0:T(8,128)(2,1)}, u32[]{:S(2)}, u32[]{:S(2)}) collective-permute-start(bf16[512,1024]{1,0:T(8,128)(2,1)} %shard_map.130), channel_id=1, source_target_pairs={{0,8},{8,0},{1,9},{9,1},{2,10},{10,2},{3,11},{11,3},{4,12},{12,4},... | collective-permute-start | bytes 3145736 | tf_op jit(solution)/shard_map/ppermute | solution.py:53
  479.2 5.9 %copy-start = (f32[256,1024]{1,0:T(8,128)S(1)}, f32[256,1024]{1,0:T(8,128)}, u32[]{:S(2)}) copy-start(f32[256,1024]{1,0:T(8,128)} %get-tuple-element.28) | copy-start | bytes 3145732

commit v2 on v0

--- a/solution.py
+++ b/solution.py
@@ -208,8 +208,8 @@
     side = total_rows // 2
     block = part.shape[1]
     layers = side // block
-    wide = width // 2
     rest = side - sure
+    edges = (0, rest // 32 * 16, rest)
     tile = half
     tiles = near_w.shape[1] * near_w.shape[2] // tile
     per = near_w.shape[2] // tile
@@ -226,17 +226,10 @@
             src_ref=source, dst_ref=target, send_sem=send, recv_sem=recv, device_id=device, device_id_type=MESH_ID
         )
 
-    def span(way):
-        return pl.ds(way * side, side)
-
     def row_copy(way, piece, step):
-        columns = pl.ds(piece * wide, wide)
+        here = pl.ds(way * side + piece * block, block)
         return remote(
-            rows.at[step - 1, span(way), columns],
-            rows.at[step, span(way), columns],
-            row_send.at[way, piece, step],
-            row_recv.at[way, piece, step],
-            ways[way],
+            rows.at[step - 1, here], rows.at[step, here], row_send.at[way, piece, step], row_recv.at[way, piece, step], ways[way]
         )
 
     def flag_copy(way, step):
@@ -245,7 +238,7 @@
         )
 
     def got_copy(way, piece):
-        here = (pl.ds(way * layers, layers), slice(None), pl.ds(piece * wide, wide))
+        here = way * layers + piece
         return remote(parcel_ref.at[here], part.at[here], got_send.at[way, piece], got_recv.at[way, piece], peer)
 
     high, deep = grad_in.shape[1], grad_in.shape[2]
@@ -265,12 +258,12 @@
         return remote(stage.at[step % 2, here], sums.at[step, here], sum_send.at[way, step], sum_recv.at[way, step], ways[way])
 
     def rest_copy(way, half_index, step):
-        here = pl.ds(way * rest, rest)
-        there = pl.ds(sure + way * rest, rest)
-        columns = pl.ds(half_index * (width // 2), width // 2)
+        first, size = edges[half_index], edges[half_index + 1] - edges[half_index]
+        here = pl.ds(way * rest + first, size)
+        there = pl.ds(sure + way * rest + first, size)
         return remote(
-            stage_rest.at[step % 2, here, columns],
-            rows.at[step, there, columns],
+            stage_rest.at[step % 2, here],
+            rows.at[step, there],
             rest_send.at[way, half_index, step],
             rest_recv.at[way, half_index, step],
             ways[way],
@@ -353,19 +346,19 @@
         load.wait()
     for number in range(4):
         piece, way = number // 2, number % 2
-        columns = pl.ds(piece * wide, wide)
-        pull = local(kept_ref.at[pl.ds(way * layers, layers), :, columns], kept_in, 0)
+        layer = way * layers + piece
+        pull = local(kept_ref.at[layer], kept_in, 0)
         pull.start()
         pull.wait()
         got_copy(way, piece).wait_recv()
 
         def join(index, _):
-            place = pl.ds(pl.multiple_of(way * side + index * block, block), block)
-            value = kept_in[index] + part[way * layers + index, :, columns].astype(jnp.float32)
-            rows[0, place, columns] = value.astype(jnp.bfloat16)
+            columns = pl.ds(pl.multiple_of(index * chunk, chunk), chunk)
+            value = kept_in[:, columns] + part[layer, :, columns].astype(jnp.float32)
+            rows[0, way * side + piece * block : way * side + (piece + 1) * block, columns] = value.astype(jnp.bfloat16)
             return 0
 
-        lax.fori_loop(0, layers, join, 0)
+        lax.fori_loop(0, width // chunk, join, 0)
         row_copy(way, piece, 1).start()
         if number < 3:
             gradient_step(number + 1)
@@ -563,9 +556,8 @@
 
         for half_index in range(2):
             for way in range(2):
-                here = slice(way * rest, (way + 1) * rest)
-                there = slice(sure + way * rest, sure + (way + 1) * rest)
-                columns = slice(half_index * (width // 2), (half_index + 1) * (width // 2))
+                here = slice(way * rest + edges[half_index], way * rest + edges[half_index + 1])
+                there = slice(sure + here.start, sure + here.stop)
 
                 @pl.when(step >= 3)
                 def _():
@@ -574,13 +566,13 @@
                 @pl.when(step >= 2)
                 def _():
                     rest_copy(way, half_index, step - 1).wait_recv()
-                    stage_rest[step % 2, here, columns] = (
-                        near_w[1, 0, here, columns].astype(jnp.float32) + rows[step - 1, there, columns].astype(jnp.float32)
+                    stage_rest[step % 2, here] = (
+                        near_w[1, 0, here].astype(jnp.float32) + rows[step - 1, there].astype(jnp.float32)
                     ).astype(jnp.bfloat16)
 
                 @pl.when(step < 2)
                 def _():
-                    stage_rest[step % 2, here, columns] = near_w[1, 0, here, columns]
+                    stage_rest[step % 2, here] = near_w[1, 0, here]
 
                 @pl.when(step < count)
                 def _():
@@ -765,37 +757,30 @@
     )(routes, own.reshape(1), heads_out.reshape(strips, strip, depth), weight, tokens.reshape(strips, strip, width))
 
 
-def finish_kernel(place_ref, route_ref, front_ref, back_ref, old_ref, joined_ref, divergence_ref):
-    strip = front_ref.shape[1]
-    fresh = jnp.where(route_ref[pl.program_id(0)] >= 1, 1.0, 0.0)
-    for index, source in enumerate((front_ref, back_ref)):
-        here = slice(index * strip, (index + 1) * strip)
-        value = source[0]
-        joined_ref[0, here] = value
-        gap = value.astype(jnp.float32) - old_ref[0, here].astype(jnp.float32)
-        divergence_ref[0, here] = 0.5 * jnp.mean(gap * gap, axis=-1, keepdims=True) * fresh
-
-
-def finished(place, fresh, out, old_out, strip):
+def finish_kernel(place_ref, route_ref, out_ref, old_ref, joined_ref, divergence_ref):
+    blocks, strip = old_ref.shape[0], out_ref.shape[1]
+    for block in range(blocks):
+        fresh = jnp.where(route_ref[block] >= 1, 1.0, 0.0)
+        for index in range(2):
+            here = slice(index * strip, (index + 1) * strip)
+            value = out_ref[place_ref[index, block]]
+            joined_ref[block, here] = value
+            gap = value.astype(jnp.float32) - old_ref[block, here].astype(jnp.float32)
+            divergence_ref[block, here] = 0.5 * jnp.mean(gap * gap, axis=-1, keepdims=True) * fresh
+
+
+def finished(place, routes, out, old_out, strip):
     blocks, piece, width = old_out.shape
-    whole = pl.BlockSpec((1, piece, width), lambda i, place, fresh: (i, 0, 0))
+    smem, vmem = pl.BlockSpec(memory_space=pltpu.SMEM), pl.BlockSpec(memory_space=pltpu.VMEM)
     return pl.pallas_call(
         finish_kernel,
-        grid_spec=pltpu.PrefetchScalarGridSpec(
-            num_scalar_prefetch=2,
-            grid=(blocks,),
-            in_specs=[
-                pl.BlockSpec((1, strip, width), lambda i, place, fresh: (place[0, i], 0, 0)),
-                pl.BlockSpec((1, strip, width), lambda i, place, fresh: (place[1, i], 0, 0)),
-                whole,
-            ],
-            out_specs=[whole, pl.BlockSpec((1, piece, 1), lambda i, place, fresh: (i, 0, 0))],
-        ),
+        in_specs=[smem, smem, vmem, vmem],
+        out_specs=[vmem, vmem],
         out_shape=(
             jax.ShapeDtypeStruct((blocks, piece, width), jnp.bfloat16),
             jax.ShapeDtypeStruct((blocks, piece, 1), jnp.float32),
         ),
-    )(place, fresh, out.reshape(-1, strip, width), out.reshape(-1, strip, width), old_out)
+    )(place, routes, out.reshape(-1, strip, width), old_out)
 
 
 def two_experts(
@@ -869,7 +854,7 @@
             pltpu.VMEM((2, high, deep // 2), low),
             pltpu.VMEM((2, 2, high, deep // 2), low),
             pltpu.VMEM((high, deep), jnp.float32),
-            pltpu.VMEM((side // (2 * loose), 2 * loose, width // 2), jnp.float32),
+            pltpu.VMEM((2 * loose, width), jnp.float32),
             pltpu.VMEM((2, count, loose, 128), jnp.float32),
             dma((2, 2, count)), dma((2, 2, count)), dma((2, count)), dma((2, count)),
             dma((2, count)), dma((2, count)), dma((2, 2, count)), dma((2, 2, count)),

time: 475 us -> 472 us (level)
  no operation moved by 1% of the time
where the time goes in v2:
time: 472 us; the launch traced here: 471 us
  Pallas kernels  448 us (95%)
  matrix products  9.13 us (2%)
  local copies, waits for them, and re-layouts  7.33 us (2%)
    pallas_call x1, Pallas kernels, two_experts(): pl.pallas_call(functools.partial(moe_kernel, sure, loose, half), out_shap...  410 us
    pallas_call x1, Pallas kernels, attended(): pl.pallas_call(attend_kernel, grid=(steps,), in_specs=[pl.BlockSpec((leng...  23.7 us
    pallas_call x1, Pallas kernels, projected(): pl.pallas_call(functools.partial(project_kernel, capacity), grid_spec=plt...  10.9 us
  transfers between devices with their start and end apart: 3, of which 0 were waited for; matrix products, arithmetic and copies ran while one was open for 2% of the time, Pallas kernels for 7%

profile of v2, /device:TPU:0, one launch (start us, length us, event | category | flops | bytes accessed | tf_op | source)
XLA Modules:
  0.0 470.9 jit_solution(18225978624605799159)
XLA Ops:
  0.6 3.7 constant_dynamic-slice_fusion.3
  4.3 0.0 copy-start.1
  4.3 0.2 pad_maximum_fusion
  4.5 0.6 collective-permute-start.1
  5.0 1.3 copy-done.1
  6.3 1.4 slice_bitcast_fusion
  7.7 3.0 collective-permute-start
  10.7 23.7 %shard_map.130 = bf16[512,1024]{1,0:T(8,128)(2,1)} custom-call(bf16[512,4096]{1,0:T(8,128)(2,1)} %tokens_ref.1, bf16[4096,1024]{1,0:T(8,128)(2,1)} %query_ref.1, bf16[4096,512]{1,0:T(8,128)(2,1)} %key_ref.1, bf16[4096,512]{1,0:T(8,128)(2,1)} %value_ref.1), custom_call_target="tpu_custom_call" | custom-call | flops 8589934592 | bytes 20971520 | tf_op jit(solution)/shard_map/pallas_call | solution.py:659
  34.5 0.0 collective-permute-start.2
  34.5 10.9 %shard_map.131 = (bf16[256,4096]{1,0:T(8,128)(2,1)}, f32[256,4096]{1,0:T(8,128)}, s32[2,8]{1,0:T(2,128)}, f32[32,128]{1,0:T(8,128)}) custom-call(s32[8]{0:T(128)} %bitcast.14, s32[1]{0:T(128)} %bitcast.1.own_ref, bf16[32,16,1024]{2,1,0:T(8,128)(2,1)} %bitcast.19, bf16[1024,4096]{1,0:T(8,128)(2,1)} %weight_ref.1, bf16[32,16,4096]{2,1,0:T(8,128)(2,1)} %bitcast.16), custom_call_target="tpu_custom_call" | custom-call | flops 4294967296 | bytes 20000000 | tf_op jit(solution)/shard_map/pallas_call | solution.py:732
  45.3 0.0 collective-permute-done.2
  45.3 0.0 collective-permute-done.1
  45.3 9.1 %fusion.6.term_ref = bf16[2048,1024]{1,0:T(8,128)(2,1)} fusion(bf16[512,2048]{1,0:T(8,128)(2,1)} %collective-permute-done.1, bf16[512,1024]{1,0:T(8,128)(2,1)} %get-tuple-element.20, bf16[512,1024]{1,0:T(8,128)(2,1)S(1)} %get-tuple-element.19, bf16[512,1024]{1,0:T(8,128)(2,1)} %collective-permute-done.2, bf16[512,1024]{1,0:T(8,128)(2,1)} %shard_map.130), kind=kOutput, calls=%fused_computation.6 | convolution fusion | flops 4313841664 | bytes 10485760 | tf_op jit(solution)/shard_map/dot_general | solution.py:821
  54.5 0.0 collective-permute-done.early_ref
  54.5 409.5 %shard_map.132 = (bf16[256,4096]{1,0:T(8,128)(2,1)}, f32[256,1024]{1,0:T(8,128)}, bf16[3,2,448,4096]{3,2,1,0:T(8,128)(2,1)}, bf16[2,8,256,512]{3,2,1,0:T(8,128)(2,1)}) custom-call(bf16[4,64,4096]{2,1,0:T(8,128)(2,1)} %bitcast.21, f32[4,64,4096]{2,1,0:T(8,128)} %bitcast.20, bf16[224,4096]{1,0:T(8,128)(2,1)} %collective-permute-done.early_ref, ...), custom_call_target="tpu_custom_call" | custom-call | flops 99999997952 | bytes 100000000 | tf_op jit(solution)/shard_map/pallas_call | solution.py:832
  464.0 0.0 copy-start
  464.0 4.3 shard_map.133
  468.3 1.6 reduce
  469.9 0.0 copy-done
  469.9 1.0 copy.15
Async XLA Ops:
  4.3 2.0 copy-start.1
  4.5 40.9 %collective-permute-start.1 = (bf16[512,2048]{1,0:T(8,128)(2,1)S(1)}, bf16[512,2048]{1,0:T(8,128)(2,1)}, u32[]{:S(2)}, u32[]{:S(2)}) collective-permute-start(bf16[512,2048]{1,0:T(8,128)(2,1)S(1)} %pad_maximum_fusion), channel_id=1, source_target_pairs={{0,8},{8,0},{1,9},{9,1},{2,10},{10,2},{3,11},{11,3},{4,12},{12,4},... | collective-permute-start | bytes 6291464 | tf_op jit(solution)/shard_map/ppermute | solution.py:53
  7.7 46.7 %collective-permute-start = (bf16[224,4096]{1,0:T(8,128)(2,1)}, bf16[224,4096]{1,0:T(8,128)(2,1)}, u32[]{:S(2)}, u32[]{:S(2)}) collective-permute-start(bf16[224,4096]{1,0:T(8,128)(2,1)} %slice_bitcast_fusion), channel_id=1, source_target_pairs={{0,1},{1,0},{2,3},{3,2},{4,5},{5,4},{6,7},{7,6},{8,9},{9,8},{10,11... | collective-permute-start | bytes 5505032 | tf_op jit(solution)/shard_map/ppermute | solution.py:53
  34.5 10.9 %collective-permute-start.2 = (bf16[512,1024]{1,0:T(8,128)(2,1)}, bf16[512,1024]{1,0:T(8,128)(2,1)}, u32[]{:S(2)}, u32[]{:S(2)}) collective-permute-start(bf16[512,1024]{1,0:T(8,128)(2,1)} %shard_map.130), channel_id=1, source_target_pairs={{0,8},{8,0},{1,9},{9,1},{2,10},{10,2},{3,11},{11,3},{4,12},{12,4},... | collective-permute-start | bytes 3145736 | tf_op jit(solution)/shard_map/ppermute | solution.py:53
  464.0 5.9 %copy-start = (f32[256,1024]{1,0:T(8,128)S(1)}, f32[256,1024]{1,0:T(8,128)}, u32[]{:S(2)}) copy-start(f32[256,1024]{1,0:T(8,128)} %get-tuple-element.28) | copy-start | bytes 3145732

commit v3 on v2

--- a/solution.py
+++ b/solution.py
@@ -344,6 +344,11 @@
     early_copy().start()
     for load in loads:
         load.wait()
+
+    def pass_on(way, piece):
+        row_copy(way, piece, 1).wait_recv()
+        row_copy(way, piece, 2).start()
+
     for number in range(4):
         piece, way = number // 2, number % 2
         layer = way * layers + piece
@@ -360,8 +365,11 @@
 
         lax.fori_loop(0, width // chunk, join, 0)
         row_copy(way, piece, 1).start()
+        if number > 0:
+            pass_on((number - 1) % 2, (number - 1) // 2)
         if number < 3:
             gradient_step(number + 1)
+    pass_on(1, 1)
     for which in range(3):
         pair_copy(which).wait_recv()
 
@@ -454,7 +462,7 @@
         lax.fori_loop(0, tiles, one, 0)
 
     def ring_step(step, _):
-        @pl.when(step >= 1)
+        @pl.when(step >= 2)
         def _():
             for piece in range(2):
                 for way in range(2):
@@ -464,6 +472,8 @@
                     def _():
                         row_copy(way, piece, step + 1).start()
 
+        @pl.when(step >= 1)
+        def _():
             for way in range(2):
                 flag_copy(way, step).wait_recv()
 

time: 472 us -> 472 us (level)
  no operation moved by 1% of the time
where the time goes in v3:
time: 472 us; the launch traced here: 471 us
  Pallas kernels  449 us (95%)
  matrix products  9.13 us (2%)
  local copies, waits for them, and re-layouts  7.33 us (2%)
    pallas_call x1, Pallas kernels, two_experts(): pl.pallas_call(functools.partial(moe_kernel, sure, loose, half), out_shap...  410 us
    pallas_call x1, Pallas kernels, attended(): pl.pallas_call(attend_kernel, grid=(steps,), in_specs=[pl.BlockSpec((leng...  23.7 us
    pallas_call x1, Pallas kernels, projected(): pl.pallas_call(functools.partial(project_kernel, capacity), grid_spec=plt...  10.9 us
  transfers between devices with their start and end apart: 3, of which 0 were waited for; matrix products, arithmetic and copies ran while one was open for 2% of the time, Pallas kernels for 7%

profile of v3, /device:TPU:0, one launch (start us, length us, event | category | flops | bytes accessed | tf_op | source)
XLA Modules:
  0.0 471.4 jit_solution(6483061337833301297)
XLA Ops:
  0.6 3.7 constant_dynamic-slice_fusion.3
  4.3 0.0 copy-start.1
  4.3 0.2 pad_maximum_fusion
  4.5 0.6 collective-permute-start.1
  5.0 1.3 copy-done.1
  6.3 1.4 slice_bitcast_fusion
  7.7 3.0 collective-permute-start
  10.7 23.7 %shard_map.130 = bf16[512,1024]{1,0:T(8,128)(2,1)} custom-call(bf16[512,4096]{1,0:T(8,128)(2,1)} %tokens_ref.1, bf16[4096,1024]{1,0:T(8,128)(2,1)} %query_ref.1, bf16[4096,512]{1,0:T(8,128)(2,1)} %key_ref.1, bf16[4096,512]{1,0:T(8,128)(2,1)} %value_ref.1), custom_call_target="tpu_custom_call" | custom-call | flops 8589934592 | bytes 20971520 | tf_op jit(solution)/shard_map/pallas_call | solution.py:669
  34.5 0.0 collective-permute-start.2
  34.5 10.9 %shard_map.131 = (bf16[256,4096]{1,0:T(8,128)(2,1)}, f32[256,4096]{1,0:T(8,128)}, s32[2,8]{1,0:T(2,128)}, f32[32,128]{1,0:T(8,128)}) custom-call(s32[8]{0:T(128)} %bitcast.14, s32[1]{0:T(128)} %bitcast.1.own_ref, bf16[32,16,1024]{2,1,0:T(8,128)(2,1)} %bitcast.19, bf16[1024,4096]{1,0:T(8,128)(2,1)} %weight_ref.1, bf16[32,16,4096]{2,1,0:T(8,128)(2,1)} %bitcast.16), custom_call_target="tpu_custom_call" | custom-call | flops 4294967296 | bytes 20000000 | tf_op jit(solution)/shard_map/pallas_call | solution.py:742
  45.3 0.0 collective-permute-done.2
  45.3 0.0 collective-permute-done.1
  45.3 9.1 %fusion.6.term_ref = bf16[2048,1024]{1,0:T(8,128)(2,1)} fusion(bf16[512,2048]{1,0:T(8,128)(2,1)} %collective-permute-done.1, bf16[512,1024]{1,0:T(8,128)(2,1)} %get-tuple-element.20, bf16[512,1024]{1,0:T(8,128)(2,1)S(1)} %get-tuple-element.19, bf16[512,1024]{1,0:T(8,128)(2,1)} %collective-permute-done.2, bf16[512,1024]{1,0:T(8,128)(2,1)} %shard_map.130), kind=kOutput, calls=%fused_computation.6 | convolution fusion | flops 4313841664 | bytes 10485760 | tf_op jit(solution)/shard_map/dot_general | solution.py:831
  54.5 0.0 collective-permute-done.early_ref
  54.5 410.0 %shard_map.132 = (bf16[256,4096]{1,0:T(8,128)(2,1)}, f32[256,1024]{1,0:T(8,128)}, bf16[3,2,448,4096]{3,2,1,0:T(8,128)(2,1)}, bf16[2,8,256,512]{3,2,1,0:T(8,128)(2,1)}) custom-call(bf16[4,64,4096]{2,1,0:T(8,128)(2,1)} %bitcast.21, f32[4,64,4096]{2,1,0:T(8,128)} %bitcast.20, bf16[224,4096]{1,0:T(8,128)(2,1)} %collective-permute-done.early_ref, ...), custom_call_target="tpu_custom_call" | custom-call | flops 99999997952 | bytes 100000000 | tf_op jit(solution)/shard_map/pallas_call | solution.py:842
  464.5 0.0 copy-start
  464.5 4.3 shard_map.133
  468.8 1.6 reduce
  470.4 0.0 copy-done
  470.4 1.0 copy.15
Async XLA Ops:
  4.3 2.0 copy-start.1
  4.5 40.9 %collective-permute-start.1 = (bf16[512,2048]{1,0:T(8,128)(2,1)S(1)}, bf16[512,2048]{1,0:T(8,128)(2,1)}, u32[]{:S(2)}, u32[]{:S(2)}) collective-permute-start(bf16[512,2048]{1,0:T(8,128)(2,1)S(1)} %pad_maximum_fusion), channel_id=1, source_target_pairs={{0,8},{8,0},{1,9},{9,1},{2,10},{10,2},{3,11},{11,3},{4,12},{12,4},... | collective-permute-start | bytes 6291464 | tf_op jit(solution)/shard_map/ppermute | solution.py:53
  7.7 46.7 %collective-permute-start = (bf16[224,4096]{1,0:T(8,128)(2,1)}, bf16[224,4096]{1,0:T(8,128)(2,1)}, u32[]{:S(2)}, u32[]{:S(2)}) collective-permute-start(bf16[224,4096]{1,0:T(8,128)(2,1)} %slice_bitcast_fusion), channel_id=1, source_target_pairs={{0,1},{1,0},{2,3},{3,2},{4,5},{5,4},{6,7},{7,6},{8,9},{9,8},{10,11... | collective-permute-start | bytes 5505032 | tf_op jit(solution)/shard_map/ppermute | solution.py:53
  34.5 10.9 %collective-permute-start.2 = (bf16[512,1024]{1,0:T(8,128)(2,1)}, bf16[512,1024]{1,0:T(8,128)(2,1)}, u32[]{:S(2)}, u32[]{:S(2)}) collective-permute-start(bf16[512,1024]{1,0:T(8,128)(2,1)} %shard_map.130), channel_id=1, source_target_pairs={{0,8},{8,0},{1,9},{9,1},{2,10},{10,2},{3,11},{11,3},{4,12},{12,4},... | collective-permute-start | bytes 3145736 | tf_op jit(solution)/shard_map/ppermute | solution.py:53
  464.5 5.9 %copy-start = (f32[256,1024]{1,0:T(8,128)S(1)}, f32[256,1024]{1,0:T(8,128)}, u32[]{:S(2)}) copy-start(f32[256,1024]{1,0:T(8,128)} %get-tuple-element.28) | copy-start | bytes 3145732
